TPU v7x, 256 devices: a whole 4x4x8 slice. The times are simulated.
256 devices in a mesh: dp: 32 (over z_lo, x, core), group: 8 (over y, z_hi).
Axes of the slice: x: 4, y: 4, z: 8 (z_hi: 2, z_lo: 4; z = z_hi * 4 + z_lo), core: 2. Of those that a mesh axis runs over, the one named last changes fastest.
Arguments:
- tokens: bfloat16 [32768, 7168], P('dp', 'group'), may hold values from -6 to 6
- proj_in: bfloat16 [32, 1024, 2, 7168], P(None, 'dp', None, 'group'), may hold values from -0.0625 to 0.0625
- proj_out: bfloat16 [32, 1024, 7168], P(None, 'dp', 'group'), may hold values from -0.1875 to 0.1875
- expert_list: int32 [32, 2], replicated, may hold values from 0 to 31, as said below
- block_pattern: int32 [32, 2, 8], replicated, may hold values from 0 to 1, as said below
- route_weight: float32 [32768, 2], P('dp'), may hold values from 0.1 to 1
Outputs:
- mixed: bfloat16 [32768, 7168], P('dp', 'group')
Inputs may be any that keep to these rules, and one draw needn't show every extreme that they name: `expert_list`: each row names 2 different experts of the window. `block_pattern`: 1 where the list slot's expert acts on that block of 128 tokens, else 0; the share of ones differs from token group to token group, and in every draw some token group has every block of every slot set.
All inputs are finite; a program needn't handle non-finite values.
Results may differ from a plain program's by a relative error of at most 0.025.
Values may be sent and summed in bfloat16 or wider, within the bound.
A program may use at most 128 MiB of HBM per device.

v0:
```python
import jax
import jax.numpy as jnp
from jax import lax
from jax.sharding import PartitionSpec as P


def on_device(tokens, proj_in, proj_out, expert_list, block_pattern, route_weight):
    group_size = lax.axis_size("group")
    n_dp = lax.axis_size("dp")
    dp_index = lax.axis_index("dp")
    row_count, width_here = tokens.shape
    slots = expert_list.shape[1]
    ff_here = proj_in.shape[1]
    block_rows = row_count // block_pattern.shape[2]
    own_pattern = lax.dynamic_index_in_dim(block_pattern, dp_index, 0, keepdims=False)
    block_mask = jnp.repeat(own_pattern, block_rows, axis=1).astype(jnp.float32)
    token_scale = route_weight.T * block_mask
    send_in = jnp.take(proj_in, expert_list, axis=0).transpose(0, 1, 3, 2, 4)
    send_out = jnp.take(proj_out, expert_list, axis=0)
    gathered = []
    weights_out = []
    pending = tokens
    for slot in range(slots):
        pending, piece = lax.optimization_barrier((pending, send_in[:, slot]))
        weight_in = lax.all_to_all(piece, "dp", 0, 0, tiled=True).reshape(-1, width_here)
        partial_here = jnp.dot(weight_in, tokens.T, preferred_element_type=jnp.float32)
        partial_here = partial_here.astype(jnp.bfloat16)
        shares = lax.psum_scatter(partial_here, "group", scatter_dimension=0, tiled=True)
        gathered.append(shares)
        pending = partial_here
    for slot in range(slots):
        pending, piece = lax.optimization_barrier((pending, send_out[:, slot]))
        weight_out = lax.all_to_all(piece, "dp", 0, 0, tiled=True)
        weights_out.append(weight_out.reshape(-1, width_here))
        pending = weight_out
    combined = None
    for slot in range(slots):
        shares = (
            gathered[slot].astype(jnp.float32).reshape(n_dp // group_size, 2, ff_here, row_count)
        )
        hidden = (token_scale[slot] * jax.nn.silu(shares[:, 0]) * shares[:, 1]).astype(jnp.bfloat16)
        hidden = lax.all_gather(hidden.reshape(-1, row_count), "group", axis=0, tiled=True)
        term = lax.dot_general(
            hidden, weights_out[slot], (((0,), (0,)), ((), ())), preferred_element_type=jnp.float32
        )
        combined = term if combined is None else combined + term
    return combined.astype(jnp.bfloat16)


def solution(mesh):
    return jax.shard_map(
        on_device,
        mesh=mesh,
        in_specs=(
            P("dp", "group"),
            P(None, "dp", None, "group"),
            P(None, "dp", "group"),
            P(),
            P(),
            P("dp", None),
        ),
        out_specs=P("dp", "group"),
        check_vma=False,
    )
```

profile of v0, /device:TPU:2, one launch (start us, length us, event | category | flops | bytes accessed | tf_op | source)
XLA Modules:
  0.0 597.1 jit_solution(7984410373641122394)
XLA Ops:
  6.5 0.0 copy-start
  6.5 0.0 reduce-scatter.3.cloned.1.call-start
  6.5 0.8 compare_select_fusion
  7.4 0.7 compare_and_fusion
  8.0 0.1 copy.16
  8.1 0.1 reshape.54
  8.2 19.4 %gather_fusion = bf16[64,32,2,896]{3,2,1,0:T(2,128)(2,1)} fusion(bf16[32,32,2,896]{3,2,1,0:T(2,128)(2,1)} %param.7, s32[1024]{0:T(1024)S(1)} %pad_clamp_fusion), kind=kCustom, calls=%fused_computation | custom fusion | bytes 14680320 | tf_op jit(solution)/shard_map/jit(_take)/gather | solution.py:18
  27.7 7.7 %copy.17 = bf16[64,32,2,896]{3,1,2,0:T(8,128)(2,1)} copy(bf16[64,32,2,896]{3,2,1,0:T(2,128)(2,1)} %gather_fusion) | data formatting | bytes 14680064 | tf_op jit(solution)/shard_map/jit(_take)/gather | solution.py:18
  35.4 0.1 copy.15
  35.5 3.9 select_bitcast_fusion
  39.4 2.5 slice_bitcast_fusion
  41.9 91.0 %all_to_all.20 = bf16[32,2,32,896]{3,2,1,0:T(8,128)(2,1)S(1)} all-to-all(bf16[32,2,32,896]{3,2,1,0:T(8,128)(2,1)S(1)} %get-tuple-element.9), channel_id=1, replica_groups=mesh['dp'=32,'group'=8] {'dp'}, dimensions={0} | all-to-all | bytes 7340032 | tf_op jit(solution)/shard_map/all_to_all | solution.py:25
  132.9 0.0 copy-done
  132.9 6.3 %convolution_convert_fusion.1 = bf16[2048,1024]{1,0:T(8,128)(2,1)} fusion(bf16[2048,896]{1,0:T(8,128)(2,1)S(1)} %bitcast.76, bf16[1024,896]{1,0:T(8,128)(2,1)S(1)} %copy-done), kind=kOutput, calls=%fused_computation.4 | convolution fusion | flops 3760193536 | bytes 9699328 | tf_op jit(solution)/shard_map/dot_general | solution.py:26
  139.2 0.0 reduce-scatter.3.cloned.1.call-update
  139.2 0.0 reduce-scatter.5.cloned.1.call-start
  139.3 144.2 %all_to_all.21 = bf16[32,2,32,896]{3,2,1,0:T(8,128)(2,1)S(1)} all-to-all(bf16[32,2,32,896]{3,2,1,0:T(8,128)(2,1)} %get-tuple-element.10), channel_id=1, replica_groups=mesh['dp'=32,'group'=8] {'dp'}, dimensions={0} | all-to-all | bytes 7340032 | tf_op jit(solution)/shard_map/all_to_all | solution.py:25
  283.5 6.3 %convolution_convert_fusion = bf16[2048,1024]{1,0:T(8,128)(2,1)} fusion(bf16[2048,896]{1,0:T(8,128)(2,1)S(1)} %bitcast.77, bf16[1024,896]{1,0:T(8,128)(2,1)S(1)} %copy-done), kind=kOutput, calls=%fused_computation.3 | convolution fusion | flops 3760193536 | bytes 9699328 | tf_op jit(solution)/shard_map/dot_general | solution.py:26
  289.7 0.0 copy-start.2
  289.7 0.0 reduce-scatter.5.cloned.1.call-update
  289.8 0.0 all-gather.3.cloned.1.call-start
  289.8 1.4 copy-done.2
  291.2 0.0 copy-start.4
  291.2 0.0 copy-start.3
  291.2 2.8 gather_fusion.1
  294.0 0.0 copy-done.4
  294.0 0.2 convert_reduce_fusion
  294.2 0.1 broadcast_bitcast_fusion
  294.3 0.0 copy-done.3
  294.3 4.3 broadcast_select_fusion
  298.6 1.1 fusion.11
  299.7 0.9 fusion.5
  300.6 0.0 all-gather.3.cloned.1.call-update
  300.6 4.6 slice_bitcast_fusion.2
  305.2 5.7 all-to-all-start.2
  311.0 0.0 all-gather.5.cloned.1.call-start
  311.0 114.5 %reduce-scatter.5.cloned.1.call-done = bf16[256,1024]{1,0:T(8,128)(2,1)} async-done(((bf16[2048,1024]{1,0:T(8,128)(2,1)}), bf16[256,1024]{1,0:T(8,128)(2,1)}) %reduce-scatter.5.cloned.1.call-update) | async-done | bytes 524304 | tf_op jit(solution)/shard_map/reduce_scatter | solution.py:28
  425.5 1.1 fusion.10
  426.7 0.9 fusion
  427.5 0.0 all-gather.5.cloned.1.call-update
  427.6 0.0 all-to-all-done.2
  427.6 5.0 all-to-all-start.3
  432.6 66.5 %all-gather.3.cloned.1.call-done = bf16[1024,1024]{1,0:T(8,128)(2,1)} async-done(((bf16[128,1024]{1,0:T(8,128)(2,1)}), bf16[1024,1024]{1,0:T(8,128)(2,1)}) %all-gather.3.cloned.1.call-update) | async-done | bytes 2097168 | tf_op jit(solution)/shard_map/all_gather | solution.py:42
  499.1 6.3 %fusion.13 = f32[1024,896]{1,0:T(8,128)} fusion(bf16[1024,1024]{1,0:T(8,128)(2,1)} %all-gather.3.cloned.1.call-done, bf16[1024,896]{1,0:T(8,128)(2,1)} %bitcast.14), kind=kOutput, calls=%fused_computation.36 | convolution fusion | flops 1879048192 | bytes 7602176 | tf_op jit(solution)/shard_map/dot_general | solution.py:43
  505.4 0.0 all-to-all-done.3
  505.4 78.2 %all-gather.5.cloned.1.call-done = bf16[1024,1024]{1,0:T(8,128)(2,1)} async-done(((bf16[128,1024]{1,0:T(8,128)(2,1)}), bf16[1024,1024]{1,0:T(8,128)(2,1)}) %all-gather.5.cloned.1.call-update) | async-done | bytes 2097168 | tf_op jit(solution)/shard_map/all_gather | solution.py:42
  583.6 7.0 %add_convert_fusion = bf16[1024,896]{1,0:T(8,128)(2,1)} fusion(f32[1024,896]{1,0:T(8,128)} %fusion.13, bf16[1024,1024]{1,0:T(8,128)(2,1)} %all-gather.5.cloned.1.call-done, bf16[1024,896]{1,0:T(8,128)(2,1)} %bitcast.21), kind=kOutput, calls=%fused_computation.7 | convolution fusion | flops 1880883200 | bytes 9437184 | tf_op jit(solution)/shard_map/dot_general | solution.py:43
  590.6 0.0 copy-done.1
  (5 shorter events, 0.0 us)
Async XLA Ops:
  6.5 126.4 %copy-start = (bf16[1024,896]{1,0:T(8,128)(2,1)S(1)}, bf16[1024,896]{1,0:T(8,128)(2,1)}, u32[]{:S(2)}) copy-start(bf16[1024,896]{1,0:T(8,128)(2,1)} %param.6) | copy-start | bytes 5505028
  6.5 292.0 %reduce-scatter.3.cloned.1.call-start = ((), (), s32[]{:S(2)}) async-start(), calls=%async_computation.6 | async-start | bytes 4718592 | tf_op jit(solution)/shard_map/reduce_scatter | solution.py:28
  139.2 286.3 %reduce-scatter.5.cloned.1.call-start = ((), (), s32[]{:S(2)}) async-start(), calls=%async_computation.8 | async-start | bytes 4718592 | tf_op jit(solution)/shard_map/reduce_scatter | solution.py:28
  289.7 1.5 copy-start.2
  289.8 209.3 %all-gather.3.cloned.1.call-start = ((), (), s32[]{:S(2)}) async-start(), calls=%async_computation.7 | async-start | bytes 2359296 | tf_op jit(solution)/shard_map/all_gather | solution.py:42
  291.2 2.8 copy-start.4
  291.2 3.0 copy-start.3
  305.2 122.3 %all-to-all-start.2 = ((bf16[32,32,896]{2,1,0:T(8,128)(2,1)}), bf16[32,32,896]{2,1,0:T(8,128)(2,1)}, u32[]{:S(2)}, u32[]{:S(2)}) async-start(bf16[32,32,896]{2,1,0:T(8,128)(2,1)} %get-tuple-element.11), calls=%async_computation.3 | async-start | bytes 3670016 | tf_op jit(solution)/shard_map/all_to_all | solution.py:33
  311.0 272.6 %all-gather.5.cloned.1.call-start = ((), (), s32[]{:S(2)}) async-start(), calls=%async_computation.9 | async-start | bytes 2359296 | tf_op jit(solution)/shard_map/all_gather | solution.py:42
  427.6 77.8 %all-to-all-start.3 = ((bf16[32,32,896]{2,1,0:T(8,128)(2,1)}), bf16[32,32,896]{2,1,0:T(8,128)(2,1)}, u32[]{:S(2)}, u32[]{:S(2)}) async-start(bf16[32,32,896]{2,1,0:T(8,128)(2,1)} %get-tuple-element.12), calls=%async_computation.5 | async-start | bytes 3670016 | tf_op jit(solution)/shard_map/all_to_all | solution.py:33
  583.6 7.0 %copy-start.1 = (bf16[1024,896]{1,0:T(8,128)(2,1)S(1)}, bf16[1024,896]{1,0:T(8,128)(2,1)}, u32[]{:S(2)}) copy-start(bf16[1024,896]{1,0:T(8,128)(2,1)} %param.6) | copy-start | bytes 5505028
Sparse Core Ops, SparseCore 0:
  139.3 143.6 reduce-scatter.2
  289.9 135.5 reduce-scatter.4
  428.1 70.8 all-gather.2
  501.5 82.0 all-gather.4
where the time goes:
time: 598 us; the launch traced here: 597 us
  waiting for transfers between devices  259 us (43%)
  blocking collectives  235 us (39%)
  local copies, waits for them, and re-layouts  41.1 us (7%)
  matrix products  25.8 us (4%)
  between operations  13.2 us (2%)
  other arithmetic  11.6 us (2%)
  starting transfers between devices  10.9 us (2%)
    all_to_all x2, blocking collectives, on_device(): lax.all_to_all(piece, 'dp', 0, 0, tiled=True).reshape(-1, width_here)  235 us
    all_gather x2, waiting for transfers between devices, on_device(): lax.all_gather(hidden.reshape(-1, row_count), 'group', axis=0, tiled=True)  145 us
    reduce_scatter x2, waiting for transfers between devices, on_device(): lax.psum_scatter(partial_here, 'group', scatter_dimension=0, tiled=True)  114 us
    gather x2, local copies, waits for them, and re-layouts, on_device(): send_in = jnp.take(proj_in, expert_list, axis=0).transpose(0, 1, 3, 2, 4)  27.2 us
    dot_general x2, matrix products, on_device(): lax.dot_general(hidden, weights_out[slot], (((0,), (0,)), ((), ())), pref...  13.3 us
    dot_general x2, matrix products, on_device(): jnp.dot(weight_in, tokens.T, preferred_element_type=jnp.float32)  12.6 us
  transfers between devices with their start and end apart: 6, of which 3 were waited for; matrix products, arithmetic and copies ran while one was open for 5% of the time, Pallas kernels for 0%

commit v1 on v0

--- a/solution.py
+++ b/solution.py
@@ -39,7 +39,12 @@
             gathered[slot].astype(jnp.float32).reshape(n_dp // group_size, 2, ff_here, row_count)
         )
         hidden = (token_scale[slot] * jax.nn.silu(shares[:, 0]) * shares[:, 1]).astype(jnp.bfloat16)
-        hidden = lax.all_gather(hidden.reshape(-1, row_count), "group", axis=0, tiled=True)
+        hidden = jnp.concatenate(
+            lax.all_to_all(
+                jnp.stack([hidden.reshape(-1, row_count)] * lax.axis_size("group")), "group", 0, 0
+            ),
+            axis=0,
+        )
         term = lax.dot_general(
             hidden, weights_out[slot], (((0,), (0,)), ((), ())), preferred_element_type=jnp.float32
         )

time: 598 us -> 580 us (0.970)
  blocking collectives: 235 us -> 91 us
  waiting for transfers between devices: 259 us -> 334 us
  starting transfers between devices: 10.9 us -> 60.7 us
    all_to_all x0 -> x3, waiting for transfers between devices: none -> 217 us  [the longest x1 124 us: on_device(): lax.all_to_all(piece, 'dp', 0, 0, tiled=True).reshape(-1, width_here)]
    all_gather x2 -> x0, waiting for transfers between devices: 145 us -> none  [on_device(): lax.all_gather(hidden.reshape(-1, row_count), 'group', axis=0, tiled=True)]
    all_to_all x2 -> x1, blocking collectives: 235 us -> 91 us  [on_device(): lax.all_to_all(piece, 'dp', 0, 0, tiled=True).reshape(-1, width_here)]
    all_to_all x2, waiting for transfers between devices: 0.01 us -> 116 us  [on_device(): weight_out = lax.all_to_all(piece, 'dp', 0, 0, tiled=True)]
    reduce_scatter x2, waiting for transfers between devices: 114 us -> 0.04 us  [on_device(): lax.psum_scatter(partial_here, 'group', scatter_dimension=0, tiled=True)]
    all_to_all x0 -> x3, starting transfers between devices: none -> 31.9 us  [the longest x2 25.9 us: on_device(): lax.all_to_all(jnp.stack([hidden.reshape(-1, row_count)] * lax.axis_size(...]
    all_to_all x2, starting transfers between devices: 10.7 us -> 28.5 us  [on_device(): weight_out = lax.all_to_all(piece, 'dp', 0, 0, tiled=True)]
  transfers between devices with their start and end apart: 6 -> 7, of which waited for: 3 -> 5; matrix products, arithmetic and copies ran while one was open for 5% -> 5% of each run, Pallas kernels for 0% -> 0%
where the time goes in v1:
time: 580 us; the launch traced here: 577 us
  waiting for transfers between devices  334 us (58%)
  blocking collectives  91 us (16%)
  starting transfers between devices  60.7 us (10%)
  local copies, waits for them, and re-layouts  42 us (7%)
  matrix products  27.8 us (5%)
  between operations  13.5 us (2%)
  other arithmetic  8.35 us (1%)
    all_to_all x1, waiting for transfers between devices, on_device(): lax.all_to_all(piece, 'dp', 0, 0, tiled=True).reshape(-1, width_here)  124 us
    all_to_all x2, waiting for transfers between devices, on_device(): weight_out = lax.all_to_all(piece, 'dp', 0, 0, tiled=True)  116 us
    all_to_all x2, waiting for transfers between devices, on_device(): lax.all_to_all(jnp.stack([hidden.reshape(-1, row_count)] * lax.axis_size(...  92.8 us
    all_to_all x1, blocking collectives, on_device(): lax.all_to_all(piece, 'dp', 0, 0, tiled=True).reshape(-1, width_here)  91 us
    all_to_all x2, starting transfers between devices, on_device(): weight_out = lax.all_to_all(piece, 'dp', 0, 0, tiled=True)  28.5 us
    gather x2, local copies, waits for them, and re-layouts, on_device(): send_in = jnp.take(proj_in, expert_list, axis=0).transpose(0, 1, 3, 2, 4)  27.2 us
    all_to_all x2, starting transfers between devices, on_device(): lax.all_to_all(jnp.stack([hidden.reshape(-1, row_count)] * lax.axis_size(...  25.9 us
    dot_general x2, matrix products, on_device(): jnp.dot(weight_in, tokens.T, preferred_element_type=jnp.float32)  14.5 us
  transfers between devices with their start and end apart: 7, of which 5 were waited for; matrix products, arithmetic and copies ran while one was open for 5% of the time, Pallas kernels for 0%

profile of v1, /device:TPU:2, one launch (start us, length us, event | category | flops | bytes accessed | tf_op | source)
XLA Modules:
  0.0 577.0 jit_solution(9635242433226771777)
XLA Ops:
  6.5 0.0 copy-start
  6.5 0.8 compare_select_fusion
  7.4 0.7 compare_and_fusion
  8.0 0.1 copy.16
  8.1 0.1 reshape.66
  8.2 19.4 %gather_fusion = bf16[64,32,2,896]{3,2,1,0:T(2,128)(2,1)} fusion(bf16[32,32,2,896]{3,2,1,0:T(2,128)(2,1)} %param.7, s32[1024]{0:T(1024)S(1)} %pad_clamp_fusion), kind=kCustom, calls=%fused_computation | custom fusion | bytes 14680320 | tf_op jit(solution)/shard_map/jit(_take)/gather | solution.py:18
  27.7 7.8 %copy.17 = bf16[64,32,2,896]{3,1,2,0:T(8,128)(2,1)} copy(bf16[64,32,2,896]{3,2,1,0:T(2,128)(2,1)} %gather_fusion) | data formatting | bytes 14680064 | tf_op jit(solution)/shard_map/jit(_take)/gather | solution.py:18
  35.4 0.1 copy.15
  35.5 3.9 select_bitcast_fusion
  39.4 2.5 slice_bitcast_fusion
  41.9 91.0 %all_to_all.30 = bf16[32,2,32,896]{3,2,1,0:T(8,128)(2,1)S(1)} all-to-all(bf16[32,2,32,896]{3,2,1,0:T(8,128)(2,1)S(1)} %get-tuple-element.9), channel_id=1, replica_groups=mesh['dp'=32,'group'=8] {'dp'}, dimensions={0} | all-to-all | bytes 7340032 | tf_op jit(solution)/shard_map/all_to_all | solution.py:25
  132.9 0.0 copy-done
  132.9 6.3 %convolution_convert_fusion.1 = bf16[2048,1024]{1,0:T(8,128)(2,1)} fusion(bf16[2048,896]{1,0:T(8,128)(2,1)S(1)} %bitcast.78, bf16[1024,896]{1,0:T(8,128)(2,1)S(1)} %copy-done), kind=kOutput, calls=%fused_computation.4 | convolution fusion | flops 3760193536 | bytes 9699328 | tf_op jit(solution)/shard_map/dot_general | solution.py:26
  139.2 5.9 %all-to-all-start.2 = ((bf16[32,2,32,896]{3,2,1,0:T(8,128)(2,1)}), bf16[32,2,32,896]{3,2,1,0:T(8,128)(2,1)}, u32[]{:S(2)}, u32[]{:S(2)}) async-start(bf16[32,2,32,896]{3,2,1,0:T(8,128)(2,1)} %get-tuple-element.10), calls=%async_computation.3 | async-start | bytes 7340032 | tf_op jit(solution)/shard_map/all_to_all | solution.py:25
  145.1 0.2 reduce-scatter.3.cloned.1.call-start
  145.3 0.5 reduce-scatter.3.cloned.1.call-update
  145.8 4.3 gather_fusion.1
  150.1 2.5 broadcast_select_fusion
  152.6 2.2 slice_bitcast_fusion.2
  154.8 123.9 %all-to-all-done.2 = bf16[32,2,32,896]{3,2,1,0:T(8,128)(2,1)} async-done(((bf16[32,2,32,896]{3,2,1,0:T(8,128)(2,1)}), bf16[32,2,32,896]{3,2,1,0:T(8,128)(2,1)}, u32[]{:S(2)}, u32[]{:S(2)}) %all-to-all-start.2) | async-done | bytes 3670048 | tf_op jit(solution)/shard_map/all_to_all | solution.py:25
  278.7 8.3 %convolution_convert_fusion = bf16[2048,1024]{1,0:T(8,128)(2,1)} fusion(bf16[2048,896]{1,0:T(8,128)(2,1)} %bitcast.12, bf16[1024,896]{1,0:T(8,128)(2,1)S(1)} %copy-done), kind=kOutput, calls=%fused_computation.3 | convolution fusion | flops 3760193536 | bytes 9699328 | tf_op jit(solution)/shard_map/dot_general | solution.py:26
  287.0 0.0 copy-start.3
  287.0 8.2 %all-to-all-start.3 = ((bf16[32,32,896]{2,1,0:T(8,128)(2,1)}), bf16[32,32,896]{2,1,0:T(8,128)(2,1)}, u32[]{:S(2)}, u32[]{:S(2)}) async-start(bf16[32,32,896]{2,1,0:T(8,128)(2,1)} %get-tuple-element.11), calls=%async_computation.4 | async-start | bytes 3670016 | tf_op jit(solution)/shard_map/all_to_all | solution.py:33
  295.2 0.0 reduce-scatter.5.cloned.1.call-start
  295.2 0.7 reduce-scatter.5.cloned.1.call-update
  295.9 0.0 copy-done.3
  295.9 0.2 convert_reduce_fusion
  296.1 0.1 broadcast_bitcast_fusion
  296.2 0.0 copy-done.2
  296.2 0.0 reduce-scatter.3.cloned.1.call-done
  296.2 1.1 fusion.11
  297.4 0.2 fusion.5
  297.5 74.3 %all-to-all-done.3 = bf16[32,32,896]{2,1,0:T(8,128)(2,1)} async-done(((bf16[32,32,896]{2,1,0:T(8,128)(2,1)}), bf16[32,32,896]{2,1,0:T(8,128)(2,1)}, u32[]{:S(2)}, u32[]{:S(2)}) %all-to-all-start.3) | async-done | bytes 1835040 | tf_op jit(solution)/shard_map/all_to_all | solution.py:33
  371.8 1.6 stack.6
  373.4 21.3 %all-to-all-start.1 = ((bf16[8,128,1024]{2,1,0:T(8,128)(2,1)}), bf16[8,128,1024]{2,1,0:T(8,128)(2,1)}, u32[]{:S(2)}, u32[]{:S(2)}) async-start(bf16[8,128,1024]{2,1,0:T(8,128)(2,1)} %stack.6), calls=%async_computation.2 | async-start | bytes 4194304 | tf_op jit(solution)/shard_map/all_to_all | solution.py:43
  394.7 48.3 %all-to-all-done.1 = bf16[8,128,1024]{2,1,0:T(8,128)(2,1)} async-done(((bf16[8,128,1024]{2,1,0:T(8,128)(2,1)}), bf16[8,128,1024]{2,1,0:T(8,128)(2,1)}, u32[]{:S(2)}, u32[]{:S(2)}) %all-to-all-start.1) | async-done | bytes 2097184 | tf_op jit(solution)/shard_map/all_to_all | solution.py:43
  443.0 20.4 %all-to-all-start.5 = ((bf16[32,32,896]{2,1,0:T(8,128)(2,1)}), bf16[32,32,896]{2,1,0:T(8,128)(2,1)}, u32[]{:S(2)}, u32[]{:S(2)}) async-start(bf16[32,32,896]{2,1,0:T(8,128)(2,1)} %get-tuple-element.12), calls=%async_computation.7 | async-start | bytes 3670016 | tf_op jit(solution)/shard_map/all_to_all | solution.py:33
  463.4 0.0 reduce-scatter.5.cloned.1.call-done
  463.4 1.1 fusion.10
  464.5 0.2 fusion
  464.7 41.5 %all-to-all-done.5 = bf16[32,32,896]{2,1,0:T(8,128)(2,1)} async-done(((bf16[32,32,896]{2,1,0:T(8,128)(2,1)}), bf16[32,32,896]{2,1,0:T(8,128)(2,1)}, u32[]{:S(2)}, u32[]{:S(2)}) %all-to-all-start.5) | async-done | bytes 1835040 | tf_op jit(solution)/shard_map/all_to_all | solution.py:33
  506.2 1.6 stack.7
  507.8 4.6 all-to-all-start.4
  512.4 6.3 %fusion.13 = f32[1024,896]{1,0:T(8,128)} fusion(bf16[1024,1024]{1,0:T(8,128)(2,1)} %bitcast.10, bf16[1024,896]{1,0:T(8,128)(2,1)} %bitcast.15), kind=kOutput, calls=%fused_computation.36 | convolution fusion | flops 1879048192 | bytes 7602176 | tf_op jit(solution)/shard_map/dot_general | solution.py:48
  518.7 44.5 %all-to-all-done.4 = bf16[8,128,1024]{2,1,0:T(8,128)(2,1)} async-done(((bf16[8,128,1024]{2,1,0:T(8,128)(2,1)}), bf16[8,128,1024]{2,1,0:T(8,128)(2,1)}, u32[]{:S(2)}, u32[]{:S(2)}) %all-to-all-start.4) | async-done | bytes 2097184 | tf_op jit(solution)/shard_map/all_to_all | solution.py:43
  563.2 0.0 copy-start.1
  563.2 7.0 %add_convert_fusion = bf16[1024,896]{1,0:T(8,128)(2,1)} fusion(f32[1024,896]{1,0:T(8,128)} %fusion.13, bf16[1024,1024]{1,0:T(8,128)(2,1)} %bitcast.21, bf16[1024,896]{1,0:T(8,128)(2,1)} %bitcast.23), kind=kOutput, calls=%fused_computation.7 | convolution fusion | flops 1880883200 | bytes 9437184 | tf_op jit(solution)/shard_map/dot_general | solution.py:48
  570.2 0.0 copy-done.1
  (4 shorter events, 0.0 us)
Async XLA Ops:
  6.5 126.4 %copy-start = (bf16[1024,896]{1,0:T(8,128)(2,1)S(1)}, bf16[1024,896]{1,0:T(8,128)(2,1)}, u32[]{:S(2)}) copy-start(bf16[1024,896]{1,0:T(8,128)(2,1)} %param.6) | copy-start | bytes 5505028
  139.2 139.5 %all-to-all-start.2 = ((bf16[32,2,32,896]{3,2,1,0:T(8,128)(2,1)}), bf16[32,2,32,896]{3,2,1,0:T(8,128)(2,1)}, u32[]{:S(2)}, u32[]{:S(2)}) async-start(bf16[32,2,32,896]{3,2,1,0:T(8,128)(2,1)} %get-tuple-element.10), calls=%async_computation.3 | async-start | bytes 7340032 | tf_op jit(solution)/shard_map/all_to_all | solution.py:25
  145.1 151.1 %reduce-scatter.3.cloned.1.call-start = ((), (), s32[]{:S(2)}) async-start(), calls=%async_computation.8 | async-start | bytes 4718592 | tf_op jit(solution)/shard_map/reduce_scatter | solution.py:28
  287.0 8.9 %copy-start.3 = (s32[32,2,8]{0,2,1:T(8,128)S(1)}, s32[32,2,8]{0,2,1:T(8,128)}, u32[]{:S(2)}) copy-start(s32[32,2,8]{0,2,1:T(8,128)} %param.10) | copy-start | bytes 6148
  287.0 9.2 %copy-start.2 = (f32[1024,2]{0,1:T(2,128)S(1)}, f32[1024,2]{0,1:T(2,128)}, u32[]{:S(2)}) copy-start(f32[1024,2]{0,1:T(2,128)} %param.11) | copy-start | bytes 24580
  287.0 84.8 %all-to-all-start.3 = ((bf16[32,32,896]{2,1,0:T(8,128)(2,1)}), bf16[32,32,896]{2,1,0:T(8,128)(2,1)}, u32[]{:S(2)}, u32[]{:S(2)}) async-start(bf16[32,32,896]{2,1,0:T(8,128)(2,1)} %get-tuple-element.11), calls=%async_computation.4 | async-start | bytes 3670016 | tf_op jit(solution)/shard_map/all_to_all | solution.py:33
  295.2 168.2 %reduce-scatter.5.cloned.1.call-start = ((), (), s32[]{:S(2)}) async-start(), calls=%async_computation.9 | async-start | bytes 4718592 | tf_op jit(solution)/shard_map/reduce_scatter | solution.py:28
  373.4 69.6 %all-to-all-start.1 = ((bf16[8,128,1024]{2,1,0:T(8,128)(2,1)}), bf16[8,128,1024]{2,1,0:T(8,128)(2,1)}, u32[]{:S(2)}, u32[]{:S(2)}) async-start(bf16[8,128,1024]{2,1,0:T(8,128)(2,1)} %stack.6), calls=%async_computation.2 | async-start | bytes 4194304 | tf_op jit(solution)/shard_map/all_to_all | solution.py:43
  443.0 63.2 %all-to-all-start.5 = ((bf16[32,32,896]{2,1,0:T(8,128)(2,1)}), bf16[32,32,896]{2,1,0:T(8,128)(2,1)}, u32[]{:S(2)}, u32[]{:S(2)}) async-start(bf16[32,32,896]{2,1,0:T(8,128)(2,1)} %get-tuple-element.12), calls=%async_computation.7 | async-start | bytes 3670016 | tf_op jit(solution)/shard_map/all_to_all | solution.py:33
  507.8 55.4 %all-to-all-start.4 = ((bf16[8,128,1024]{2,1,0:T(8,128)(2,1)}), bf16[8,128,1024]{2,1,0:T(8,128)(2,1)}, u32[]{:S(2)}, u32[]{:S(2)}) async-start(bf16[8,128,1024]{2,1,0:T(8,128)(2,1)} %stack.7), calls=%async_computation.6 | async-start | bytes 4194304 | tf_op jit(solution)/shard_map/all_to_all | solution.py:43
  563.2 7.0 %copy-start.1 = (bf16[1024,896]{1,0:T(8,128)(2,1)S(1)}, bf16[1024,896]{1,0:T(8,128)(2,1)}, u32[]{:S(2)}) copy-start(bf16[1024,896]{1,0:T(8,128)(2,1)} %param.6) | copy-start | bytes 5505028
Sparse Core Ops, SparseCore 0:
  150.1 138.1 reduce-scatter.2
  300.2 153.4 reduce-scatter.4
